TPU v7x, 32 devices: a whole 2x2x4 slice. The times are simulated.
32 devices in a mesh: dp: 2 (over x), row: 4 (over z), col: 4 (over y, core).
Axes of the slice: x: 2, y: 2, z: 4, core: 2. Of those that a mesh axis runs over, the one named last changes fastest.
Arguments:
- block_in: float32 [2048, 1152], P(('dp', 'col'), 'row'), may hold values from -6 to 6
- labels: int32 [2], P('dp'), may hold values from 0 to 1000
- steps_t: int32 [2], P('dp'), may hold values from 0 to 999
- out_cot: float32 [2048, 1152], P(('dp', 'col'), 'row'), may hold values from -6 to 6
- class_table: float32 [1001, 1152], P(None, 'col'), may hold values from -6 to 6
- w_ada: float32 [1152, 6, 1152], P('col', None, 'row'), may hold values from -0.1875 to 0.1875
- b_ada: float32 [6, 1152], P(None, 'row'), may hold values from -3 to 3
- w_qkv: float32 [1152, 3, 1152], P('row', None, 'col'), may hold values from -0.125 to 0.125
- b_qv: float32 [2, 1152], P(None, 'col'), may hold values from -3 to 3
- w_out: float32 [1152, 1152], P('col', 'row'), may hold values from -3.5 to 3.5
- b_out: float32 [1152], P('row'), may hold values from -3 to 3
- w_up: float32 [1152, 4608], P('row', 'col'), may hold values from -0.1875 to 0.1875
- b_up: float32 [4608], P('col'), may hold values from -3 to 3
- w_down: float32 [4608, 1152], P('col', 'row'), may hold values from -0.09375 to 0.09375
- b_down: float32 [1152], P('row'), may hold values from -3 to 3
Outputs:
- block_out: float32 [2048, 1152], P(('dp', 'col'), 'row')
- in_grad: float32 [2048, 1152], P(('dp', 'col'), 'row')
- table_grad: float32 [1001, 1152], P(None, 'col')
- ada_grad: float32 [1152, 6, 1152], P('col', None, 'row')
- ada_bias_grad: float32 [6, 1152], P(None, 'row')
- qkv_grad: float32 [1152, 3, 1152], P('row', None, 'col')
- qv_bias_grad: float32 [2, 1152], P(None, 'col')
- out_grad: float32 [1152, 1152], P('col', 'row')
- out_bias_grad: float32 [1152], P('row')
- up_grad: float32 [1152, 4608], P('row', 'col')
- up_bias_grad: float32 [4608], P('col')
- down_grad: float32 [4608, 1152], P('col', 'row')
- down_bias_grad: float32 [1152], P('row')
All inputs are finite; a program needn't handle non-finite values.
Results may differ from a plain program's by a relative error of at most 0.0003.
Values sent between devices are 32-bit elements; how exact they have to be, the bound alone decides.
No kernel may reach another device: no remote copies, remote signals or barrier semaphores. Data moves between devices by JAX's collectives and lax.ppermute only.
A program may use at most 128 MiB of HBM per device.

v0:
```python
from functools import partial
import math
import jax
import jax.numpy as jnp
from jax import lax
from jax.sharding import PartitionSpec as P

D = 1152
HD = 72
SEQ = 1024
exact_mode = lax.Precision.HIGHEST
norm_epsilon = 1e-06


def matmul(left, right):
    return jnp.dot(left, right, precision=exact_mode, preferred_element_type=jnp.float32)


def inner_rows(left, right):
    return lax.dot_general(
        left,
        right,
        (((0,), (0,)), ((), ())),
        precision=exact_mode,
        preferred_element_type=jnp.float32,
    )


def gather_col(local):
    return lax.all_gather(local, "col", axis=0, tiled=True)


def gather_row(local):
    return lax.all_gather(local, "row", axis=0, tiled=True)


def gather_keys(local):
    return lax.all_gather(local, "row", axis=0, tiled=True)


def project_up(local, matrix):
    gathered = gather_col(local)
    own_rows = gathered.shape[0] // lax.axis_size("row")

    def partial_term(start, row_count):
        return matmul(gathered, matrix)

    return (
        gathered,
        lax.psum_scatter(
            partial_term(jnp.int32(0), own_rows * lax.axis_size("row")),
            "row",
            scatter_dimension=0,
            tiled=True,
        ),
    )


def project_down(local, matrix):
    gathered = gather_row(local)
    own_rows = gathered.shape[0] // lax.axis_size("col")

    def partial_term(start, row_count):
        return matmul(lax.dynamic_slice_in_dim(gathered, start, row_count, 0), matrix)

    return (
        gathered,
        lax.psum_scatter(
            partial_term(jnp.int32(0), own_rows * lax.axis_size("col")),
            "col",
            scatter_dimension=0,
            tiled=True,
        ),
    )


def width_total(values):
    return lax.psum(jnp.sum(values, axis=1, keepdims=True), "row")


def width_pair(first, second):
    return lax.psum(
        (jnp.sum(first, axis=1, keepdims=True), jnp.sum(second, axis=1, keepdims=True)), "row"
    )


def normalize(values):
    center = width_total(values) / D
    centred = values - center
    spread = width_total(centred * centred) / D
    inverse = lax.rsqrt(spread + norm_epsilon)
    return (centred * inverse, inverse)


def normalize_back(grad_values, normed, inverse):
    totals, along = width_pair(grad_values, grad_values * normed)
    return inverse * (grad_values - totals / D - normed * (along / D))


def attend(queries, keyvals):
    query_rows, head_count, head_dim = queries.shape
    block_rows = min(query_rows, 512)
    factor = 1.0 / math.sqrt(head_dim)

    def attend_block(index):
        scores = jnp.einsum("qhd,khd->hqk", queries, keyvals[:, 0], precision=exact_mode) * factor
        weights = jnp.exp(scores)
        row_sums = jnp.sum(weights, axis=2, keepdims=True)
        result = jnp.einsum("hqk,khd->qhd", weights / row_sums, keyvals[:, 1], precision=exact_mode)
        return (result, jnp.log(row_sums[:, :, 0]))

    results, log_sums = lax.map(attend_block, jnp.arange(query_rows // block_rows))
    return (results.reshape(query_rows, head_count, head_dim), log_sums)


def attend_back(queries, keyvals, attended, log_sums, d_attended):
    query_rows, head_count, head_dim = queries.shape
    block_rows = min(query_rows, 512)
    factor = 1.0 / math.sqrt(head_dim)

    def back_block(kv_totals, scan_item):
        index, block_logs = scan_item
        scores = jnp.einsum("qhd,khd->hqk", queries, keyvals[:, 0], precision=exact_mode) * factor
        weights = jnp.exp(scores - block_logs[:, :, None])
        d_weights = jnp.einsum("qhd,khd->hqk", d_attended, keyvals[:, 1], precision=exact_mode)
        row_dots = jnp.transpose(jnp.sum(d_attended * attended, axis=2))
        d_scores = weights * (d_weights - row_dots[:, :, None]) * factor
        d_query = jnp.einsum("hqk,khd->qhd", d_scores, keyvals[:, 0], precision=exact_mode)
        d_key = jnp.einsum("hqk,qhd->khd", d_scores, queries, precision=exact_mode)
        d_value = jnp.einsum("hqk,qhd->khd", weights, d_attended, precision=exact_mode)
        current = kv_totals
        kv_totals = current + jnp.stack([d_key, d_value], axis=1)
        return (kv_totals, d_query)

    kv_grads, d_queries = lax.scan(
        back_block, jnp.zeros_like(keyvals), (jnp.arange(query_rows // block_rows), log_sums)
    )
    return (d_queries.reshape(query_rows, head_count, head_dim), kv_grads)


def shards(
    block_in,
    labels,
    steps_t,
    out_cot,
    class_table,
    w_ada,
    b_ada,
    w_qkv,
    b_qv,
    w_out,
    b_out,
    w_up,
    b_up,
    w_down,
    b_down,
):
    tok_local, width_row = block_in.shape
    width_col = w_out.shape[0]
    latent_count = labels.shape[0]
    head_local = width_col // HD
    label_hot = (labels[:, None] == jnp.arange(class_table.shape[0])[None, :]).astype(jnp.float32)
    feature = lax.axis_index("col") * width_col + jnp.arange(width_col)
    half_width = D // 2
    frequency = jnp.exp(
        -math.log(10000.0) * (feature % half_width).astype(jnp.float32) / half_width
    )
    angles = steps_t.astype(jnp.float32)[:, None] * frequency[None, :]
    condition = matmul(label_hot, class_table) + jnp.where(
        feature[None, :] < half_width, jnp.cos(angles), jnp.sin(angles)
    )
    silu_cond, silu_pull = jax.vjp(jax.nn.silu, condition)
    ada_terms = jnp.einsum("lc,cjr->ljr", silu_cond, w_ada, precision=exact_mode)
    modulation = lax.psum(ada_terms, "col") + b_ada
    token_index = lax.axis_index("col") * tok_local + jnp.arange(tok_local)
    member = (token_index[:, None] // SEQ == jnp.arange(latent_count)[None, :]).astype(jnp.float32)
    per_token = matmul(member, modulation.reshape(latent_count, 6 * width_row)).reshape(
        tok_local, 6, width_row
    )
    shift_one = per_token[:, 0]
    scale_one = per_token[:, 1]
    gate_one = per_token[:, 2]
    shift_two = per_token[:, 3]
    scale_two = per_token[:, 4]
    gate_two = per_token[:, 5]
    normed_one, inverse_one = normalize(block_in)
    hidden_one = normed_one * (1.0 + scale_one) + shift_one
    qkv_matrix = w_qkv.reshape(width_row, 3 * width_col)
    hidden_one_seen, qkv_local = project_up(hidden_one, qkv_matrix)
    query_rows = qkv_local.shape[0]
    qkv_local = qkv_local.reshape(query_rows, 3, width_col)
    queries = (qkv_local[:, 0] + b_qv[0]).reshape(query_rows, head_local, HD)
    keyval_local = jnp.stack([qkv_local[:, 1], qkv_local[:, 2] + b_qv[1]], axis=1)
    keyval_seen = gather_keys(keyval_local).reshape(-1, 2, head_local, HD)
    attended, log_sums = attend(queries, keyval_seen)
    attended_flat = attended.reshape(query_rows, width_col)
    attended_seen, proj_local = project_down(attended_flat, w_out)
    attn_out = proj_local + b_out
    mixed = block_in + gate_one * attn_out
    normed_two, inverse_two = normalize(mixed)
    hidden_two = normed_two * (1.0 + scale_two) + shift_two
    hidden_two_seen, up_local = project_up(hidden_two, w_up)
    activated, gelu_pull = jax.vjp(partial(jax.nn.gelu, approximate=True), up_local + b_up)
    activated_seen, down_local = project_down(activated, w_down)
    mlp_out = down_local + b_down
    block_out = mixed + gate_two * mlp_out
    hidden_one_all = gather_col(hidden_one)
    keyval_all = gather_keys(keyval_local).reshape(-1, 2, head_local, HD)
    attended_all = gather_row(attended_flat)
    hidden_two_all = gather_col(hidden_two)
    activated_all = gather_row(activated)
    d_mlp = out_cot * gate_two
    d_mlp_all, d_activated = project_up(d_mlp, w_down.T)
    (d_up,) = gelu_pull(d_activated)
    down_grad = inner_rows(activated_all, d_mlp_all)
    down_bias_grad = jnp.sum(d_mlp_all, axis=0)
    d_up_all, d_hidden_two = project_down(d_up, w_up.T)
    up_grad = inner_rows(hidden_two_all, d_up_all)
    up_bias_grad = jnp.sum(d_up_all, axis=0)
    d_mixed = out_cot + normalize_back(d_hidden_two * (1.0 + scale_two), normed_two, inverse_two)
    d_attn = d_mixed * gate_one
    d_attn_all, d_attended = project_up(d_attn, w_out.T)
    out_grad = inner_rows(attended_all, d_attn_all)
    out_bias_grad = jnp.sum(d_attn_all, axis=0)
    d_queries, kv_grads = attend_back(
        queries, keyval_all, attended, log_sums, d_attended.reshape(query_rows, head_local, HD)
    )
    kv_local_grad = lax.psum_scatter(
        kv_grads.reshape(-1, 2, width_col), "row", scatter_dimension=0, tiled=True
    )
    d_qkv = jnp.stack(
        [d_queries.reshape(query_rows, width_col), kv_local_grad[:, 0], kv_local_grad[:, 1]], axis=1
    ).reshape(query_rows, 3 * width_col)
    d_qkv_all, d_hidden_one = project_down(d_qkv, qkv_matrix.T)
    qkv_grad = inner_rows(hidden_one_all, d_qkv_all).reshape(width_row, 3, width_col)
    qv_bias_grad = jnp.stack(
        [jnp.sum(d_qkv_all[:, :width_col], axis=0), jnp.sum(d_qkv_all[:, 2 * width_col :], axis=0)]
    )
    in_grad = d_mixed + normalize_back(d_hidden_one * (1.0 + scale_one), normed_one, inverse_one)
    mod_terms = jnp.stack(
        [
            d_hidden_one,
            d_hidden_one * normed_one,
            d_mixed * attn_out,
            d_hidden_two,
            d_hidden_two * normed_two,
            out_cot * mlp_out,
        ],
        axis=1,
    )
    latent_terms = inner_rows(member, mod_terms.reshape(tok_local, 6 * width_row)).reshape(
        latent_count, 6, width_row
    )
    mod_grads = lax.psum(latent_terms, "col")
    ada_grad = jnp.einsum("lc,ljr->cjr", silu_cond, mod_grads, precision=exact_mode)
    ada_bias_grad = jnp.sum(mod_grads, axis=0)
    silu_grads = lax.psum(jnp.einsum("ljr,cjr->lc", mod_grads, w_ada, precision=exact_mode), "row")
    (cond_grad,) = silu_pull(silu_grads)
    table_grad = inner_rows(label_hot, cond_grad)
    summed = lax.psum(
        (
            table_grad,
            ada_grad,
            ada_bias_grad,
            qkv_grad,
            qv_bias_grad,
            out_grad,
            out_bias_grad,
            up_grad,
            up_bias_grad,
            down_grad,
            down_bias_grad,
        ),
        "dp",
    )
    return (
        block_out,
        in_grad,
        summed[0],
        summed[1],
        summed[2],
        summed[3],
        summed[4],
        summed[5],
        summed[6],
        summed[7],
        summed[8],
        summed[9],
        summed[10],
    )


def solution(mesh):
    in_specs = (
        P(("dp", "col"), "row"),
        P("dp"),
        P("dp"),
        P(("dp", "col"), "row"),
        P(None, "col"),
        P("col", None, "row"),
        P(None, "row"),
        P("row", None, "col"),
        P(None, "col"),
        P("col", "row"),
        P("row"),
        P("row", "col"),
        P("col"),
        P("col", "row"),
        P("row"),
    )
    out_specs = (
        P(("dp", "col"), "row"),
        P(("dp", "col"), "row"),
        P(None, "col"),
        P("col", None, "row"),
        P(None, "row"),
        P("row", None, "col"),
        P(None, "col"),
        P("col", "row"),
        P("row"),
        P("row", "col"),
        P("col"),
        P("col", "row"),
        P("row"),
    )
    return jax.shard_map(shards, mesh=mesh, in_specs=in_specs, out_specs=out_specs, check_vma=False)
```

profile of v0, /device:TPU:0, one launch (start us, length us, event | category | flops | bytes accessed | tf_op | source)
XLA Modules:
  0.0 1210.4 jit_solution(3974382097439372623)
XLA Ops:
  9.7 13.5 %psum.155 = f32[256,1]{0,1:T(1,128)S(1)} all-reduce(f32[256,1]{0,1:T(1,128)S(1)} %bitcast.212), channel_id=1, replica_groups=mesh['dp'=2,'row'=4,'col'=4] {'row'}, use_global_device_ids=true, to_apply=%region_2.3 | all-reduce | flops 256 | bytes 2048 | tf_op jit(solution)/shard_map/psum | solution.py:78
  37.3 10.3 psum.154
  52.8 14.3 %all-gather.10.cloned.1.call-done = f32[1024,288]{0,1:T(8,128)} async-done(((f32[256,288]{0,1:T(8,128)}), f32[1024,288]{0,1:T(8,128)}) %all-gather.10.cloned.1.call-update) | async-done | bytes 1179664 | tf_op jit(solution)/shard_map/all_gather | solution.py:30
  67.1 8.7 fusion.55
  76.5 66.0 %reduce-scatter.10.cloned.1.call-done = f32[256,864]{0,1:T(8,128)} async-done(((f32[1024,864]{0,1:T(8,128)}), f32[256,864]{0,1:T(8,128)}) %reduce-scatter.10.cloned.1.call-update) | async-done | bytes 884752 | tf_op jit(solution)/shard_map/reduce_scatter | solution.py:50
  145.0 50.0 %all-gather.12.cloned.1.call-done = f32[1024,2,288]{0,2,1:T(8,128)} async-done(((f32[256,2,288]{0,2,1:T(8,128)}), f32[1024,2,288]{0,2,1:T(8,128)}) %all-gather.12.cloned.1.call-update) | async-done | bytes 2359312 | tf_op jit(solution)/shard_map/all_gather | solution.py:38
  206.0 29.1 %all-gather.14.cloned.1.call-done = f32[1024,288]{0,1:T(8,128)} async-done(((f32[256,288]{0,1:T(8,128)}), f32[1024,288]{0,1:T(8,128)}) %all-gather.14.cloned.1.call-update) | async-done | bytes 1179664 | tf_op jit(solution)/shard_map/all_gather | solution.py:34
  239.6 24.9 %reduce-scatter.12.cloned.1.call-done = f32[256,288]{0,1:T(8,128)} async-done(((f32[1024,288]{0,1:T(8,128)}), f32[256,288]{0,1:T(8,128)}) %reduce-scatter.12.cloned.1.call-update) | async-done | bytes 294928 | tf_op jit(solution)/shard_map/reduce_scatter | solution.py:68
  265.7 11.7 psum.157
  277.4 8.9 psum.158
  290.1 15.3 %all-gather.16.cloned.1.call-done = f32[1024,288]{0,1:T(8,128)} async-done(((f32[256,288]{0,1:T(8,128)}), f32[1024,288]{0,1:T(8,128)}) %all-gather.16.cloned.1.call-update) | async-done | bytes 1179664 | tf_op jit(solution)/shard_map/all_gather | solution.py:30
  305.4 11.1 fusion.57
  325.0 11.2 fusion.59
  336.2 76.4 %reduce-scatter.14.cloned.1.call-done = f32[256,1152]{1,0:T(8,128)} async-done(((f32[1024,1152]{1,0:T(8,128)}), f32[256,1152]{1,0:T(8,128)}) %reduce-scatter.14.cloned.1.call-update) | async-done | bytes 1179664 | tf_op jit(solution)/shard_map/reduce_scatter | solution.py:50
  412.6 88.2 %reduce-scatter.18.cloned.1.call-done = f32[256,1152]{1,0:T(8,128)} async-done(((f32[1024,1152]{1,0:T(8,128)}), f32[256,1152]{1,0:T(8,128)}) %reduce-scatter.18.cloned.1.call-update) | async-done | bytes 1179664 | tf_op jit(solution)/shard_map/reduce_scatter | solution.py:50
  505.8 88.9 %all-gather.22.cloned.1.call-done = f32[1024,1152]{1,0:T(8,128)} async-done(((f32[256,1152]{1,0:T(8,128)}), f32[1024,1152]{1,0:T(8,128)}) %all-gather.22.cloned.1.call-update) | async-done | bytes 4718608 | tf_op jit(solution)/shard_map/all_gather | solution.py:34
  594.7 8.8 fusion.60
  603.6 81.1 %all-gather.18.cloned.1.call-done = f32[1024,1152]{1,0:T(8,128)} async-done(((f32[256,1152]{1,0:T(8,128)}), f32[1024,1152]{1,0:T(8,128)}) %all-gather.18.cloned.1.call-update) | async-done | bytes 4718608 | tf_op jit(solution)/shard_map/all_gather | solution.py:34
  684.7 8.8 fusion.58
  693.6 18.2 %reduce-scatter.20.cloned.1.call-done = f32[256,288]{0,1:T(8,128)} async-done(((f32[1024,288]{0,1:T(8,128)}), f32[256,288]{0,1:T(8,128)}) %reduce-scatter.20.cloned.1.call-update) | async-done | bytes 294928 | tf_op jit(solution)/shard_map/reduce_scatter | solution.py:68
  713.4 12.4 %all-reduce.1 = (f32[256,1]{0,1:T(1,128)}, f32[256,1]{0,1:T(1,128)}) all-reduce(f32[256,1]{0,1:T(1,128)} %bitcast.211, f32[256,1]{0,1:T(1,128)} %bitcast.210), channel_id=1, replica_groups=mesh['dp'=2,'row'=4,'col'=4] {'row'}, use_global_device_ids=true, to_apply=%region_19.20 | all-reduce | flops 512 | bytes 4096 | tf_op jit(solution)/shard_map/psum | solution.py:82
  727.1 13.4 %reduce-scatter.16.cloned.1.call-done = f32[256,288]{0,1:T(8,128)} async-done(((f32[1024,288]{0,1:T(8,128)}), f32[256,288]{0,1:T(8,128)}) %reduce-scatter.16.cloned.1.call-update) | async-done | bytes 294928 | tf_op jit(solution)/shard_map/reduce_scatter | solution.py:68
  743.2 17.3 %all-gather.24.cloned.1.call-done = f32[1024,288]{0,1:T(8,128)} async-done(((f32[256,288]{0,1:T(8,128)}), f32[1024,288]{0,1:T(8,128)}) %all-gather.24.cloned.1.call-update) | async-done | bytes 1179664 | tf_op jit(solution)/shard_map/all_gather | solution.py:30
  765.7 28.7 %reduce-scatter.22.cloned.1.call-done = f32[256,288]{0,1:T(8,128)} async-done(((f32[1024,288]{0,1:T(8,128)}), f32[256,288]{0,1:T(8,128)}) %reduce-scatter.22.cloned.1.call-update) | async-done | bytes 294928 | tf_op jit(solution)/shard_map/reduce_scatter | solution.py:50
  818.1 39.6 %reduce-scatter.24.cloned.1.call-done = f32[256,2,288]{0,2,1:T(8,128)} async-done(((f32[1024,2,288]{0,2,1:T(8,128)}), f32[256,2,288]{0,2,1:T(8,128)}) %reduce-scatter.24.cloned.1.call-update) | async-done | bytes 589840 | tf_op jit(solution)/shard_map/reduce_scatter | solution.py:228
  859.9 69.3 %all-gather.26.cloned.1.call-done = f32[1024,864]{0,1:T(8,128)} async-done(((f32[256,864]{0,1:T(8,128)}), f32[1024,864]{0,1:T(8,128)}) %all-gather.26.cloned.1.call-update) | async-done | bytes 3538960 | tf_op jit(solution)/shard_map/all_gather | solution.py:34
  938.4 9.1 fusion.66
  947.5 8.5 fusion.65
  970.1 10.5 psum.163
  985.7 10.3 all-reduce
  1007.8 10.3 all-reduce.2
  1021.3 170.0 %all-reduce.6.cloned.1.call-done = (f32[1001,288]{0,1:T(8,128)}, f32[288,6,288]{2,0,1:T(8,128)}, f32[288,3,288]{0,2,1:T(8,128)}, f32[288,288]{1,0:T(8,128)}, f32[288,1152]{1,0:T(8,128)}, /*index=5*/f32[1152,288]{0,1:T(8,128)}) async-done(((f32[1001,288]{0,1:T(8,128)}, f32[288,6,288]{2,0,1:T(8,128)}, f32[288,3,288]{0,2,1:T(8,128)}, f32[288,288]{1,0:T(8,128)}, f32[288,1152]{1,0:T(8,128)}, ...) | async-done | bytes 7125136 | tf_op jit(solution)/shard_map/psum | solution.py:260
  (214 shorter events, 149.6 us)
Async XLA Ops:
  7.2 28.7 %copy-start = (f32[288,6,288]{2,0,1:T(8,128)S(1)}, f32[288,6,288]{2,0,1:T(8,128)}, u32[]{:S(2)}) copy-start(f32[288,6,288]{2,0,1:T(8,128)} %param.20) | copy-start | bytes 5971972
  7.2 59.9 %all-gather.10.cloned.1.call-start = ((), (), s32[]{:S(2)}) async-start(), calls=%async_computation.9 | async-start | bytes 1474560 | tf_op jit(solution)/shard_map/all_gather | solution.py:30
  32.6 15.2 %copy-start.28 = (f32[256,1]{0,1:T(1,128)}, f32[256,1]{0,1:T(1,128)S(1)}, u32[]{:S(2)}) copy-start(f32[256,1]{0,1:T(1,128)S(1)} %add_rsqrt_fusion.1) | copy-start | bytes 3076
  49.8 92.6 %reduce-scatter.10.cloned.1.call-start = ((), (), s32[]{:S(2)}) async-start(), calls=%async_computation.10 | async-start | bytes 4423680 | tf_op jit(solution)/shard_map/reduce_scatter | solution.py:50
  75.8 119.2 %all-gather.12.cloned.1.call-start = ((), (), s32[]{:S(2)}) async-start(), calls=%async_computation.11 | async-start | bytes 2949120 | tf_op jit(solution)/shard_map/all_gather | solution.py:38
  143.7 56.9 %copy-start.17 = (f32[256,1,288]{0,2,1:T(8,128)}, f32[256,1,288]{0,2,1:T(8,128)S(1)}, u32[]{:S(2)}) copy-start(f32[256,1,288]{0,2,1:T(8,128)S(1)} %get-tuple-element.100) | copy-start | bytes 884740
  144.6 90.5 %all-gather.14.cloned.1.call-start = ((), (), s32[]{:S(2)}) async-start(), calls=%async_computation.12 | async-start | bytes 1474560 | tf_op jit(solution)/shard_map/all_gather | solution.py:34
  145.0 55.7 %copy-start.31 = (f32[4,72]{1,0:T(4,128)}, f32[4,72]{1,0:T(4,128)S(1)}, u32[]{:S(2)}) copy-start(f32[4,72]{1,0:T(4,128)S(1)} %add.211) | copy-start | bytes 3460
  200.7 34.4 %copy-start.21 = (f32[288,288]{1,0:T(8,128)S(1)}, f32[288,288]{1,0:T(8,128)}, u32[]{:S(2)}) copy-start(f32[288,288]{1,0:T(8,128)} %param.24) | copy-start | bytes 995332
  205.9 58.6 %copy-start.40 = (f32[288]{0:T(512)S(1)}, f32[288]{0:T(512)}, u32[]{:S(2)}) copy-start(f32[288]{0:T(512)} %param.25) | copy-start | bytes 3460
  205.9 58.6 %reduce-scatter.12.cloned.1.call-start = ((), (), s32[]{:S(2)}) async-start(), calls=%async_computation.13 | async-start | bytes 1474560 | tf_op jit(solution)/shard_map/reduce_scatter | solution.py:68
  239.5 47.6 %copy-start.14 = (f32[256,288]{0,1:T(8,128)S(1)}, f32[256,288]{0,1:T(8,128)}, u32[]{:S(2)}) copy-start(f32[256,288]{0,1:T(8,128)} %param.18) | copy-start | bytes 884740
  239.5 65.9 %all-gather.16.cloned.1.call-start = ((), (), s32[]{:S(2)}) async-start(), calls=%async_computation.14 | async-start | bytes 1474560 | tf_op jit(solution)/shard_map/all_gather | solution.py:30
  289.1 35.9 %all-gather.20.cloned.1.call-start = ((), (), s32[]{:S(2)}) async-start(), calls=%async_computation.18 | async-start | bytes 1474560 | tf_op jit(solution)/shard_map/all_gather | solution.py:30
  289.9 122.7 %reduce-scatter.14.cloned.1.call-start = ((), (), s32[]{:S(2)}) async-start(), calls=%async_computation.15 | async-start | bytes 5898240 | tf_op jit(solution)/shard_map/reduce_scatter | solution.py:50
  316.5 184.2 %reduce-scatter.18.cloned.1.call-start = ((), (), s32[]{:S(2)}) async-start(), calls=%async_computation.19 | async-start | bytes 5898240 | tf_op jit(solution)/shard_map/reduce_scatter | solution.py:50
  336.2 258.5 %all-gather.22.cloned.1.call-start = ((), (), s32[]{:S(2)}) async-start(), calls=%async_computation.20 | async-start | bytes 5898240 | tf_op jit(solution)/shard_map/all_gather | solution.py:34
  504.7 180.0 %all-gather.18.cloned.1.call-start = ((), (), s32[]{:S(2)}) async-start(), calls=%async_computation.16 | async-start | bytes 5898240 | tf_op jit(solution)/shard_map/all_gather | solution.py:34
  505.4 206.4 %reduce-scatter.20.cloned.1.call-start = ((), (), s32[]{:S(2)}) async-start(), calls=%async_computation.21 | async-start | bytes 1474560 | tf_op jit(solution)/shard_map/reduce_scatter | solution.py:68
  603.5 137.0 %reduce-scatter.16.cloned.1.call-start = ((), (), s32[]{:S(2)}) async-start(), calls=%async_computation.17 | async-start | bytes 1474560 | tf_op jit(solution)/shard_map/reduce_scatter | solution.py:68
  693.5 47.0 %copy-start.42 = (f32[288]{0:T(512)S(1)}, f32[288]{0:T(512)}, u32[]{:S(2)}) copy-start(f32[288]{0:T(512)} %param.29) | copy-start | bytes 3460
  693.5 67.0 %all-gather.24.cloned.1.call-start = ((), (), s32[]{:S(2)}) async-start(), calls=%async_computation.22 | async-start | bytes 1474560 | tf_op jit(solution)/shard_map/all_gather | solution.py:30
  742.9 51.5 %copy-start.26 = (f32[4,72,256]{2,1,0:T(8,128)S(1)}, f32[4,72,256]{2,1,0:T(8,128)}, u32[]{:S(2)}) copy-start(f32[4,72,256]{2,1,0:T(8,128)} %fusion) | copy-start | bytes 884740
  742.9 51.5 %reduce-scatter.22.cloned.1.call-start = ((), (), s32[]{:S(2)}) async-start(), calls=%async_computation.23 | async-start | bytes 1474560 | tf_op jit(solution)/shard_map/reduce_scatter | solution.py:50
  765.0 92.8 %reduce-scatter.24.cloned.1.call-start = ((), (), s32[]{:S(2)}) async-start(), calls=%async_computation.24 | async-start | bytes 2949120 | tf_op jit(solution)/shard_map/reduce_scatter | solution.py:228
  811.2 118.0 %all-gather.26.cloned.1.call-start = ((), (), s32[]{:S(2)}) async-start(), calls=%async_computation.25 | async-start | bytes 4423680 | tf_op jit(solution)/shard_map/all_gather | solution.py:34
  859.8 106.0 %reduce-scatter.26.cloned.1.call-start = ((), (), s32[]{:S(2)}) async-start(), calls=%async_computation.26 | async-start | bytes 1474560 | tf_op jit(solution)/shard_map/reduce_scatter | solution.py:68
  936.7 254.5 %all-reduce.6.cloned.1.call-start = ((), (), s32[]{:S(2)}) async-start(), calls=%async_computation.27 | async-start | bytes 16515072 | tf_op jit(solution)/shard_map/psum | solution.py:260
  982.4 13.6 %copy-start.36 = (f32[288]{0:T(512)S(1)}, f32[288]{0:T(512)}, u32[]{:S(2)}) copy-start(f32[288]{0:T(512)} %copy-done.35) | copy-start | bytes 3460
  982.4 13.6 %copy-start.44 = (f32[288]{0:T(512)S(1)}, f32[288]{0:T(512)}, u32[]{:S(2)}) copy-start(f32[288]{0:T(512)} %get-tuple-element.89) | copy-start | bytes 3460
  982.4 13.6 %copy-start.37 = (f32[1,1001]{1,0:T(1,128)S(1)}, f32[1,1001]{1,0:T(1,128)}, u32[]{:S(2)}) copy-start(f32[1,1001]{1,0:T(1,128)} %compare_convert_fusion) | copy-start | bytes 12016
  1005.3 14.1 %copy-start.20 = (f32[256,288]{0,1:T(8,128)S(1)}, f32[256,288]{0,1:T(8,128)}, u32[]{:S(2)}) copy-start(f32[256,288]{0,1:T(8,128)} %get-tuple-element.92) | copy-start | bytes 884740
  (35 other events, 171.1 us)
Sparse Core Ops, SparseCore 0:
  49.9 17.1 all-gather.9
  75.9 66.4 reduce-scatter.9
  144.8 50.1 all-gather.11
  206.0 29.0 all-gather.13
  239.6 24.8 reduce-scatter.11
  289.2 16.1 all-gather.15
  307.5 17.4 all-gather.19
  327.3 85.2 reduce-scatter.13
  414.9 85.7 reduce-scatter.17
  504.8 89.8 all-gather.21
  596.9 87.7 all-gather.17
  687.7 24.0 reduce-scatter.19
  714.9 25.5 reduce-scatter.15
  743.0 17.4 all-gather.23
  765.1 29.3 reduce-scatter.21
  811.4 46.3 reduce-scatter.23
  859.9 69.2 all-gather.25
  936.8 24.1 reduce-scatter.25
  997.4 193.8 all-reduce.5
where the time goes:
time: 1220 us; the launch traced here: 1210 us
  waiting for transfers between devices  901 us (74%)
  matrix products  130 us (11%)
  blocking collectives  96.1 us (8%)
  other arithmetic  44 us (4%)
  local copies, waits for them, and re-layouts  20.7 us (2%)
  between operations  16.1 us (1%)
    all_gather x4, waiting for transfers between devices, gather_row(): return lax.all_gather(local, 'row', axis=0, tiled=True)  268 us
    reduce_scatter x4, waiting for transfers between devices, project_up(): lax.psum_scatter(partial_term(jnp.int32(0), own_rows * lax.axis_size('row...  259 us
    psum x1, waiting for transfers between devices, shards(): lax.psum((table_grad, ada_grad, ada_bias_grad, qkv_grad, qv_bias_grad, ou...  170 us
    dot_general x9, matrix products, matmul(): jnp.dot(left, right, precision=exact_mode, preferred_element_type=jnp.flo...  66.8 us
    reduce_scatter x4, waiting for transfers between devices, project_down(): lax.psum_scatter(partial_term(jnp.int32(0), own_rows * lax.axis_size('col...  56.6 us
    all_gather x4, waiting for transfers between devices, gather_col(): return lax.all_gather(local, 'col', axis=0, tiled=True)  55.3 us
    all_gather x1, waiting for transfers between devices, gather_keys(): return lax.all_gather(local, 'row', axis=0, tiled=True)  50 us
    psum x4, blocking collectives, width_total(): return lax.psum(jnp.sum(values, axis=1, keepdims=True), 'row')  42.4 us
  transfers between devices with their start and end apart: 19, of which 18 were waited for; matrix products, arithmetic and copies ran while one was open for 8% of the time, Pallas kernels for 0%

commit v1 on v0

--- a/solution.py
+++ b/solution.py
@@ -10,6 +10,19 @@
 SEQ = 1024
 exact_mode = lax.Precision.HIGHEST
 norm_epsilon = 1e-06
+
+
+def gather_around(array, axis, dim):
+    ways = lax.axis_size(axis)
+    up = [(d, (d + 1) % ways) for d in range(ways)]
+    down = [(d, (d - 1) % ways) for d in range(ways)]
+    earlier, later = ([array], [array])
+    for _ in range(ways // 2):
+        earlier.append(lax.ppermute(earlier[-1], axis, up))
+    for _ in range((ways - 1) // 2):
+        later.append(lax.ppermute(later[-1], axis, down))
+    line = jnp.concatenate([*earlier[::-1], *later[1:]], axis=dim)
+    return jnp.roll(line, (lax.axis_index(axis) - ways // 2) * array.shape[dim], axis=dim)
 
 
 def matmul(left, right):
@@ -31,7 +44,7 @@
 
 
 def gather_row(local):
-    return lax.all_gather(local, "row", axis=0, tiled=True)
+    return gather_around(local, "row", 0)
 
 
 def gather_keys(local):

time: 1220 us -> 1170 us (0.959)
  waiting for transfers between devices: 901 us -> 800 us
  starting transfers between devices: 2.36 us -> 44.3 us
  other arithmetic: 44 us -> 56.6 us
    all_gather x4 -> x0, waiting for transfers between devices: 268 us -> none  [gather_row(): return lax.all_gather(local, 'row', axis=0, tiled=True)]
    ppermute x0 -> x12, waiting for transfers between devices: none -> 182 us  [the longest x8 155 us: gather_around(): earlier.append(lax.ppermute(earlier[-1], axis, up))]
    ppermute x0 -> x12, starting transfers between devices: none -> 42.4 us  [the longest x8 29.1 us: gather_around(): earlier.append(lax.ppermute(earlier[-1], axis, up))]
    reduce_scatter x4, waiting for transfers between devices: 56.6 us -> 39.4 us  [project_down(): lax.psum_scatter(partial_term(jnp.int32(0), own_rows * lax.axis_size('col...]
    unnamed x105 -> x118, local copies, waits for them, and re-layouts: 19.3 us -> 28 us
  transfers between devices with their start and end apart: 19 -> 27, of which waited for: 18 -> 26; matrix products, arithmetic and copies ran while one was open for 8% -> 9% of each run, Pallas kernels for 0% -> 0%
where the time goes in v1:
time: 1170 us; the launch traced here: 1160 us
  waiting for transfers between devices  800 us (68%)
  matrix products  121 us (10%)
  blocking collectives  97.7 us (8%)
  other arithmetic  56.6 us (5%)
  starting transfers between devices  44.3 us (4%)
  local copies, waits for them, and re-layouts  28.9 us (2%)
  between operations  16.2 us (1%)
    reduce_scatter x4, waiting for transfers between devices, project_up(): lax.psum_scatter(partial_term(jnp.int32(0), own_rows * lax.axis_size('row...  260 us
    psum x1, waiting for transfers between devices, shards(): lax.psum((table_grad, ada_grad, ada_bias_grad, qkv_grad, qv_bias_grad, ou...  173 us
    ppermute x8, waiting for transfers between devices, gather_around(): earlier.append(lax.ppermute(earlier[-1], axis, up))  155 us
    dot_general x9, matrix products, matmul(): jnp.dot(left, right, precision=exact_mode, preferred_element_type=jnp.flo...  57.8 us
    all_gather x4, waiting for transfers between devices, gather_col(): return lax.all_gather(local, 'col', axis=0, tiled=True)  55.6 us
    all_gather x1, waiting for transfers between devices, gather_keys(): return lax.all_gather(local, 'row', axis=0, tiled=True)  50 us
    psum x4, blocking collectives, width_total(): return lax.psum(jnp.sum(values, axis=1, keepdims=True), 'row')  42.5 us
    reduce_scatter x4, waiting for transfers between devices, project_down(): lax.psum_scatter(partial_term(jnp.int32(0), own_rows * lax.axis_size('col...  39.4 us
  transfers between devices with their start and end apart: 27, of which 26 were waited for; matrix products, arithmetic and copies ran while one was open for 9% of the time, Pallas kernels for 0%

profile of v1, /device:TPU:0, one launch (start us, length us, event | category | flops | bytes accessed | tf_op | source)
XLA Modules:
  0.0 1164.9 jit_solution(13116228403729882474)
XLA Ops:
  9.7 13.5 %psum.155 = f32[256,1]{0,1:T(1,128)S(1)} all-reduce(f32[256,1]{0,1:T(1,128)S(1)} %bitcast.214), channel_id=1, replica_groups=mesh['dp'=2,'row'=4,'col'=4] {'row'}, use_global_device_ids=true, to_apply=%region_2.3 | all-reduce | flops 256 | bytes 2048 | tf_op jit(solution)/shard_map/psum | solution.py:91
  37.8 10.1 psum.154
  53.3 14.3 %all-gather.6.cloned.1.call-done = f32[1024,288]{0,1:T(8,128)} async-done(((f32[256,288]{0,1:T(8,128)}), f32[1024,288]{0,1:T(8,128)}) %all-gather.6.cloned.1.call-update) | async-done | bytes 1179664 | tf_op jit(solution)/shard_map/all_gather | solution.py:43
  77.0 66.0 %reduce-scatter.10.cloned.1.call-done = f32[256,864]{0,1:T(8,128)} async-done(((f32[1024,864]{0,1:T(8,128)}), f32[256,864]{0,1:T(8,128)}) %reduce-scatter.10.cloned.1.call-update) | async-done | bytes 884752 | tf_op jit(solution)/shard_map/reduce_scatter | solution.py:63
  145.4 50.0 %all-gather.8.cloned.1.call-done = f32[1024,2,288]{0,2,1:T(8,128)} async-done(((f32[256,2,288]{0,2,1:T(8,128)}), f32[1024,2,288]{0,2,1:T(8,128)}) %all-gather.8.cloned.1.call-update) | async-done | bytes 2359312 | tf_op jit(solution)/shard_map/all_gather | solution.py:51
  236.7 23.8 %reduce-scatter.12.cloned.1.call-done = f32[256,288]{0,1:T(8,128)} async-done(((f32[1024,288]{0,1:T(8,128)}), f32[256,288]{0,1:T(8,128)}) %reduce-scatter.12.cloned.1.call-update) | async-done | bytes 294928 | tf_op jit(solution)/shard_map/reduce_scatter | solution.py:81
  262.2 11.8 %psum.157 = f32[256,1]{0,1:T(1,128)S(1)} all-reduce(f32[256,1]{0,1:T(1,128)} %bitcast.219), channel_id=1, replica_groups=mesh['dp'=2,'row'=4,'col'=4] {'row'}, use_global_device_ids=true, to_apply=%region_9.11 | all-reduce | flops 256 | bytes 2048 | tf_op jit(solution)/shard_map/psum | solution.py:91
  274.1 8.9 psum.158
  286.6 15.4 %all-gather.10.cloned.1.call-done = f32[1024,288]{0,1:T(8,128)} async-done(((f32[256,288]{0,1:T(8,128)}), f32[1024,288]{0,1:T(8,128)}) %all-gather.10.cloned.1.call-update) | async-done | bytes 1179664 | tf_op jit(solution)/shard_map/all_gather | solution.py:43
  302.0 11.1 fusion.86
  321.5 11.2 fusion.88
  332.8 76.4 %reduce-scatter.14.cloned.1.call-done = f32[256,1152]{1,0:T(8,128)} async-done(((f32[1024,1152]{1,0:T(8,128)}), f32[256,1152]{1,0:T(8,128)}) %reduce-scatter.14.cloned.1.call-update) | async-done | bytes 1179664 | tf_op jit(solution)/shard_map/reduce_scatter | solution.py:63
  409.1 88.1 %reduce-scatter.18.cloned.1.call-done = f32[256,1152]{1,0:T(8,128)} async-done(((f32[1024,1152]{1,0:T(8,128)}), f32[256,1152]{1,0:T(8,128)}) %reduce-scatter.18.cloned.1.call-update) | async-done | bytes 1179664 | tf_op jit(solution)/shard_map/reduce_scatter | solution.py:63
  506.1 25.4 %collective-permute-done.6 = f32[256,1152]{1,0:T(8,128)S(1)} collective-permute-done((f32[256,1152]{1,0:T(8,128)S(1)}, f32[256,1152]{1,0:T(8,128)S(1)}, u32[]{:S(2)}, u32[]{:S(2)}) %collective-permute-start.6) | collective-permute-done | bytes 1179680 | tf_op jit(solution)/shard_map/ppermute | solution.py:21
  535.3 21.5 %collective-permute-done.3 = f32[256,1152]{1,0:T(8,128)} collective-permute-done((f32[256,1152]{1,0:T(8,128)}, f32[256,1152]{1,0:T(8,128)}, u32[]{:S(2)}, u32[]{:S(2)}) %collective-permute-start.3) | collective-permute-done | bytes 1179680 | tf_op jit(solution)/shard_map/ppermute | solution.py:21
  556.8 24.7 %collective-permute-start.4 = (f32[256,1152]{1,0:T(8,128)}, f32[256,1152]{1,0:T(8,128)}, u32[]{:S(2)}, u32[]{:S(2)}) collective-permute-start(f32[256,1152]{1,0:T(8,128)} %collective-permute-done.3), channel_id=1, source_target_pairs={{0,4},{4,8},{8,12},{12,0},{1,5},{5,9},{9,13},{13,1},{2,6},{6,10},{... | collective-permute-start | bytes 3538952 | tf_op jit(solution)/shard_map/ppermute | solution.py:21
  582.1 25.3 %collective-permute-done.7 = f32[256,1152]{1,0:T(8,128)S(1)} collective-permute-done((f32[256,1152]{1,0:T(8,128)S(1)}, f32[256,1152]{1,0:T(8,128)S(1)}, u32[]{:S(2)}, u32[]{:S(2)}) %collective-permute-start.7) | collective-permute-done | bytes 1179680 | tf_op jit(solution)/shard_map/ppermute | solution.py:21
  623.8 8.7 collective-permute-done.5
  632.5 24.2 %collective-permute-done.4 = f32[256,1152]{1,0:T(8,128)} collective-permute-done((f32[256,1152]{1,0:T(8,128)}, f32[256,1152]{1,0:T(8,128)}, u32[]{:S(2)}, u32[]{:S(2)}) %collective-permute-start.4) | collective-permute-done | bytes 1179680 | tf_op jit(solution)/shard_map/ppermute | solution.py:21
  675.0 12.4 %all-reduce.1 = (f32[256,1]{0,1:T(1,128)}, f32[256,1]{0,1:T(1,128)}) all-reduce(f32[256,1]{0,1:T(1,128)} %bitcast.213, f32[256,1]{0,1:T(1,128)} %bitcast.212), channel_id=1, replica_groups=mesh['dp'=2,'row'=4,'col'=4] {'row'}, use_global_device_ids=true, to_apply=%region_19.22 | all-reduce | flops 512 | bytes 4096 | tf_op jit(solution)/shard_map/psum | solution.py:95
  688.6 13.3 %reduce-scatter.16.cloned.1.call-done = f32[256,288]{0,1:T(8,128)} async-done(((f32[1024,288]{0,1:T(8,128)}), f32[256,288]{0,1:T(8,128)}) %reduce-scatter.16.cloned.1.call-update) | async-done | bytes 294928 | tf_op jit(solution)/shard_map/reduce_scatter | solution.py:81
  704.4 17.5 %all-gather.14.cloned.1.call-done = f32[1024,288]{0,1:T(8,128)} async-done(((f32[256,288]{0,1:T(8,128)}), f32[1024,288]{0,1:T(8,128)}) %all-gather.14.cloned.1.call-update) | async-done | bytes 1179664 | tf_op jit(solution)/shard_map/all_gather | solution.py:43
  726.7 29.2 %reduce-scatter.22.cloned.1.call-done = f32[256,288]{0,1:T(8,128)} async-done(((f32[1024,288]{0,1:T(8,128)}), f32[256,288]{0,1:T(8,128)}) %reduce-scatter.22.cloned.1.call-update) | async-done | bytes 294928 | tf_op jit(solution)/shard_map/reduce_scatter | solution.py:63
  779.8 39.4 %reduce-scatter.24.cloned.1.call-done = f32[256,2,288]{0,2,1:T(8,128)} async-done(((f32[1024,2,288]{0,2,1:T(8,128)}), f32[256,2,288]{0,2,1:T(8,128)}) %reduce-scatter.24.cloned.1.call-update) | async-done | bytes 589840 | tf_op jit(solution)/shard_map/reduce_scatter | solution.py:241
  821.2 22.0 %collective-permute-done.9 = f32[256,864]{0,1:T(8,128)S(1)} collective-permute-done((f32[256,864]{0,1:T(8,128)S(1)}, f32[256,864]{0,1:T(8,128)S(1)}, u32[]{:S(2)}, u32[]{:S(2)}) %collective-permute-start.9) | collective-permute-done | bytes 884768 | tf_op jit(solution)/shard_map/ppermute | solution.py:21
  847.0 20.5 %collective-permute-done.10 = f32[256,864]{0,1:T(8,128)S(1)} collective-permute-done((f32[256,864]{0,1:T(8,128)S(1)}, f32[256,864]{0,1:T(8,128)S(1)}, u32[]{:S(2)}, u32[]{:S(2)}) %collective-permute-start.10) | collective-permute-done | bytes 884768 | tf_op jit(solution)/shard_map/ppermute | solution.py:21
  867.9 14.4 %collective-permute-done.11 = f32[256,864]{0,1:T(8,128)S(1)} collective-permute-done((f32[256,864]{0,1:T(8,128)S(1)}, f32[256,864]{0,1:T(8,128)S(1)}, u32[]{:S(2)}, u32[]{:S(2)}) %collective-permute-start.11) | collective-permute-done | bytes 884768 | tf_op jit(solution)/shard_map/ppermute | solution.py:23
  892.4 8.9 fusion.92
  924.4 10.2 psum.163
  939.7 11.1 all-reduce
  958.8 11.4 all-reduce.2
  973.3 173.0 %all-reduce.6.cloned.1.call-done = (f32[1001,288]{0,1:T(8,128)}, f32[288,6,288]{2,0,1:T(8,128)}, f32[288,3,288]{0,2,1:T(8,128)}, f32[288,288]{1,0:T(8,128)}, f32[288,1152]{1,0:T(8,128)}, /*index=5*/f32[1152,288]{0,1:T(8,128)}) async-done(((f32[1001,288]{0,1:T(8,128)}, f32[288,6,288]{2,0,1:T(8,128)}, f32[288,3,288]{0,2,1:T(8,128)}, f32[288,288]{1,0:T(8,128)}, f32[288,1152]{1,0:T(8,128)}, ...) | async-done | bytes 7125136 | tf_op jit(solution)/shard_map/psum | solution.py:273
  (243 shorter events, 235.0 us)
Async XLA Ops:
  7.2 60.4 %all-gather.6.cloned.1.call-start = ((), (), s32[]{:S(2)}) async-start(), calls=%async_computation.9 | async-start | bytes 1474560 | tf_op jit(solution)/shard_map/all_gather | solution.py:43
  32.6 888.3 %copy-start.31 = (f32[256,1]{0,1:T(1,128)}, f32[256,1]{0,1:T(1,128)S(1)}, u32[]{:S(2)}) copy-start(f32[256,1]{0,1:T(1,128)S(1)} %add_rsqrt_fusion.1) | copy-start | bytes 3076
  50.3 92.6 %reduce-scatter.10.cloned.1.call-start = ((), (), s32[]{:S(2)}) async-start(), calls=%async_computation.10 | async-start | bytes 4423680 | tf_op jit(solution)/shard_map/reduce_scatter | solution.py:63
  76.3 119.2 %all-gather.8.cloned.1.call-start = ((), (), s32[]{:S(2)}) async-start(), calls=%async_computation.11 | async-start | bytes 2949120 | tf_op jit(solution)/shard_map/all_gather | solution.py:51
  144.2 56.9 %copy-start.23 = (f32[256,1,288]{0,2,1:T(8,128)}, f32[256,1,288]{0,2,1:T(8,128)S(1)}, u32[]{:S(2)}) copy-start(f32[256,1,288]{0,2,1:T(8,128)S(1)} %get-tuple-element.104) | copy-start | bytes 884740
  145.1 115.4 %reduce-scatter.12.cloned.1.call-start = ((), (), s32[]{:S(2)}) async-start(), calls=%async_computation.12 | async-start | bytes 1474560 | tf_op jit(solution)/shard_map/reduce_scatter | solution.py:81
  145.4 55.7 %copy-start.33 = (f32[4,72]{1,0:T(4,128)}, f32[4,72]{1,0:T(4,128)S(1)}, u32[]{:S(2)}) copy-start(f32[4,72]{1,0:T(4,128)S(1)} %add.236) | copy-start | bytes 3460
  206.9 12.0 %collective-permute-start = (f32[256,288]{0,1:T(8,128)}, f32[256,288]{0,1:T(8,128)}, u32[]{:S(2)}, u32[]{:S(2)}) collective-permute-start(f32[256,288]{0,1:T(8,128)} %bitcast.19), channel_id=1, source_target_pairs={{0,4},{4,8},{8,12},{12,0},{1,5},{5,9},{9,13},{13,1},{2,6},{6,10},{... | collective-permute-start | bytes 884744 | tf_op jit(solution)/shard_map/ppermute | solution.py:21
  206.9 15.3 %collective-permute-start.2 = (f32[256,288]{0,1:T(8,128)}, f32[256,288]{0,1:T(8,128)}, u32[]{:S(2)}, u32[]{:S(2)}) collective-permute-start(f32[256,288]{0,1:T(8,128)} %bitcast.19), channel_id=1, source_target_pairs={{0,12},{4,0},{8,4},{12,8},{1,13},{5,1},{9,5},{13,9},{2,14},{6,2},{... | collective-permute-start | bytes 884744 | tf_op jit(solution)/shard_map/ppermute | solution.py:23
  218.9 11.4 collective-permute-start.1
  236.6 47.1 %copy-start.20 = (f32[256,288]{0,1:T(8,128)S(1)}, f32[256,288]{0,1:T(8,128)}, u32[]{:S(2)}) copy-start(f32[256,288]{0,1:T(8,128)} %param.22) | copy-start | bytes 884740
  236.6 65.4 %all-gather.10.cloned.1.call-start = ((), (), s32[]{:S(2)}) async-start(), calls=%async_computation.13 | async-start | bytes 1474560 | tf_op jit(solution)/shard_map/all_gather | solution.py:43
  285.8 35.7 %all-gather.12.cloned.1.call-start = ((), (), s32[]{:S(2)}) async-start(), calls=%async_computation.16 | async-start | bytes 1474560 | tf_op jit(solution)/shard_map/all_gather | solution.py:43
  286.4 122.8 %reduce-scatter.14.cloned.1.call-start = ((), (), s32[]{:S(2)}) async-start(), calls=%async_computation.14 | async-start | bytes 5898240 | tf_op jit(solution)/shard_map/reduce_scatter | solution.py:63
  313.2 184.1 %reduce-scatter.18.cloned.1.call-start = ((), (), s32[]{:S(2)}) async-start(), calls=%async_computation.17 | async-start | bytes 5898240 | tf_op jit(solution)/shard_map/reduce_scatter | solution.py:63
  332.7 340.6 %reduce-scatter.20.cloned.1.call-start = ((), (), s32[]{:S(2)}) async-start(), calls=%async_computation.18 | async-start | bytes 1474560 | tf_op jit(solution)/shard_map/reduce_scatter | solution.py:81
  500.7 30.7 %collective-permute-start.6 = (f32[256,1152]{1,0:T(8,128)S(1)}, f32[256,1152]{1,0:T(8,128)S(1)}, u32[]{:S(2)}, u32[]{:S(2)}) collective-permute-start(f32[256,1152]{1,0:T(8,128)S(1)} %get-tuple-element.102), channel_id=1, source_target_pairs={{0,4},{4,8},{8,12},{12,0},{1,5},{5,9},{9,13},{13,1},{2,6},{6,10},{... | collective-permute-start | bytes 3538952 | tf_op jit(solution)/shard_map/ppermute | solution.py:21
  502.2 115.3 %copy-start.15 = (f32[288,1152]{1,0:T(8,128)S(1)}, f32[288,1152]{1,0:T(8,128)}, u32[]{:S(2)}) copy-start(f32[288,1152]{1,0:T(8,128)} %param.30) | copy-start | bytes 3981316
  502.2 54.6 %collective-permute-start.3 = (f32[256,1152]{1,0:T(8,128)}, f32[256,1152]{1,0:T(8,128)}, u32[]{:S(2)}, u32[]{:S(2)}) collective-permute-start(f32[256,1152]{1,0:T(8,128)} %get-tuple-element.103), channel_id=1, source_target_pairs={{0,4},{4,8},{8,12},{12,0},{1,5},{5,9},{9,13},{13,1},{2,6},{6,10},{... | collective-permute-start | bytes 3538952 | tf_op jit(solution)/shard_map/ppermute | solution.py:21
  504.2 77.8 %collective-permute-start.8 = (f32[256,1152]{1,0:T(8,128)S(1)}, f32[256,1152]{1,0:T(8,128)S(1)}, u32[]{:S(2)}, u32[]{:S(2)}) collective-permute-start(f32[256,1152]{1,0:T(8,128)S(1)} %get-tuple-element.102), channel_id=1, source_target_pairs={{0,12},{4,0},{8,4},{12,8},{1,13},{5,1},{9,5},{13,9},{2,14},{6,2},{... | collective-permute-start | bytes 3538952 | tf_op jit(solution)/shard_map/ppermute | solution.py:23
  531.5 75.8 %collective-permute-start.7 = (f32[256,1152]{1,0:T(8,128)S(1)}, f32[256,1152]{1,0:T(8,128)S(1)}, u32[]{:S(2)}, u32[]{:S(2)}) collective-permute-start(f32[256,1152]{1,0:T(8,128)S(1)} %collective-permute-done.6), channel_id=1, source_target_pairs={{0,4},{4,8},{8,12},{12,0},{1,5},{5,9},{9,13},{13,1},{2,6},{6,10},{... | collective-permute-start | bytes 3538952 | tf_op jit(solution)/shard_map/ppermute | solution.py:21
  531.5 101.0 %collective-permute-start.5 = (f32[256,1152]{1,0:T(8,128)}, f32[256,1152]{1,0:T(8,128)}, u32[]{:S(2)}, u32[]{:S(2)}) collective-permute-start(f32[256,1152]{1,0:T(8,128)} %get-tuple-element.103), channel_id=1, source_target_pairs={{0,12},{4,0},{8,4},{12,8},{1,13},{5,1},{9,5},{13,9},{2,14},{6,2},{... | collective-permute-start | bytes 3538952 | tf_op jit(solution)/shard_map/ppermute | solution.py:23
  556.8 100.0 %collective-permute-start.4 = (f32[256,1152]{1,0:T(8,128)}, f32[256,1152]{1,0:T(8,128)}, u32[]{:S(2)}, u32[]{:S(2)}) collective-permute-start(f32[256,1152]{1,0:T(8,128)} %collective-permute-done.3), channel_id=1, source_target_pairs={{0,4},{4,8},{8,12},{12,0},{1,5},{5,9},{9,13},{13,1},{2,6},{6,10},{... | collective-permute-start | bytes 3538952 | tf_op jit(solution)/shard_map/ppermute | solution.py:21
  623.6 78.3 %reduce-scatter.16.cloned.1.call-start = ((), (), s32[]{:S(2)}) async-start(), calls=%async_computation.15 | async-start | bytes 1474560 | tf_op jit(solution)/shard_map/reduce_scatter | solution.py:81
  671.0 51.0 %all-gather.14.cloned.1.call-start = ((), (), s32[]{:S(2)}) async-start(), calls=%async_computation.19 | async-start | bytes 1474560 | tf_op jit(solution)/shard_map/all_gather | solution.py:43
  704.4 51.5 %reduce-scatter.22.cloned.1.call-start = ((), (), s32[]{:S(2)}) async-start(), calls=%async_computation.20 | async-start | bytes 1474560 | tf_op jit(solution)/shard_map/reduce_scatter | solution.py:63
  726.4 92.8 %reduce-scatter.24.cloned.1.call-start = ((), (), s32[]{:S(2)}) async-start(), calls=%async_computation.21 | async-start | bytes 2949120 | tf_op jit(solution)/shard_map/reduce_scatter | solution.py:241
  772.8 147.1 %reduce-scatter.26.cloned.1.call-start = ((), (), s32[]{:S(2)}) async-start(), calls=%async_computation.22 | async-start | bytes 1474560 | tf_op jit(solution)/shard_map/reduce_scatter | solution.py:81
  820.3 22.8 %collective-permute-start.9 = (f32[256,864]{0,1:T(8,128)S(1)}, f32[256,864]{0,1:T(8,128)S(1)}, u32[]{:S(2)}, u32[]{:S(2)}) collective-permute-start(f32[256,864]{0,1:T(8,128)S(1)} %bitcast.168), channel_id=1, source_target_pairs={{0,4},{4,8},{8,12},{12,0},{1,5},{5,9},{9,13},{13,1},{2,6},{6,10},{... | collective-permute-start | bytes 2654216 | tf_op jit(solution)/shard_map/ppermute | solution.py:21
  843.2 24.3 %collective-permute-start.10 = (f32[256,864]{0,1:T(8,128)S(1)}, f32[256,864]{0,1:T(8,128)S(1)}, u32[]{:S(2)}, u32[]{:S(2)}) collective-permute-start(f32[256,864]{0,1:T(8,128)S(1)} %collective-permute-done.9), channel_id=1, source_target_pairs={{0,4},{4,8},{8,12},{12,0},{1,5},{5,9},{9,13},{13,1},{2,6},{6,10},{... | collective-permute-start | bytes 2654216 | tf_op jit(solution)/shard_map/ppermute | solution.py:21
  843.2 39.1 %collective-permute-start.11 = (f32[256,864]{0,1:T(8,128)S(1)}, f32[256,864]{0,1:T(8,128)S(1)}, u32[]{:S(2)}, u32[]{:S(2)}) collective-permute-start(f32[256,864]{0,1:T(8,128)S(1)} %bitcast.169), channel_id=1, source_target_pairs={{0,12},{4,0},{8,4},{12,8},{1,13},{5,1},{9,5},{13,9},{2,14},{6,2},{... | collective-permute-start | bytes 2654216 | tf_op jit(solution)/shard_map/ppermute | solution.py:23
  891.0 255.3 %all-reduce.6.cloned.1.call-start = ((), (), s32[]{:S(2)}) async-start(), calls=%async_computation.23 | async-start | bytes 16515072 | tf_op jit(solution)/shard_map/psum | solution.py:273
  (46 other events, 401.0 us)
Sparse Core Ops, SparseCore 0:
  50.4 17.1 all-gather.5
  76.4 66.4 reduce-scatter.9
  145.3 50.1 all-gather.7
  236.7 23.7 reduce-scatter.11
  285.9 16.1 all-gather.9
  304.0 17.4 all-gather.11
  323.8 85.2 reduce-scatter.13
  411.4 85.7 reduce-scatter.17
  623.7 49.5 reduce-scatter.19
  676.3 25.6 reduce-scatter.15
  704.5 17.4 all-gather.13
  726.6 29.3 reduce-scatter.21
  772.9 46.2 reduce-scatter.23
  891.2 25.6 reduce-scatter.25
  952.1 194.1 all-reduce.5
